TPU v7x, 32 devices: a whole 2x2x4 slice. The times are simulated.
32 devices in a mesh: ctx: 8 (over y, x, core), head: 4 (over z).
Axes of the slice: x: 2, y: 2, z: 4, core: 2. Of those that a mesh axis runs over, the one named last changes fastest.
Arguments:
- queries: bfloat16 [2048, 4096], P('ctx', 'head'), may hold values from -6 to 6
- key_rows: bfloat16 [2048, 4096], P('ctx', 'head'), may hold values from -6 to 6
- value_rows: bfloat16 [2048, 4096], P('ctx', 'head'), may hold values from -6 to 6
- out_weight: bfloat16 [4096, 4096], P('head'), may hold values from -0.125 to 0.125
- cotangent: bfloat16 [2048, 4096], P('ctx', 'head'), may hold values from -6 to 6
Outputs:
- mixed: bfloat16 [2048, 4096], P('ctx', 'head')
- grad_queries: bfloat16 [2048, 4096], P('ctx', 'head')
- grad_keys: bfloat16 [2048, 4096], P('ctx', 'head')
- grad_values: bfloat16 [2048, 4096], P('ctx', 'head')
- grad_out_weight: float32 [4096, 4096], P('head', 'ctx')
All inputs are finite; a program needn't handle non-finite values.
Results may differ from a plain program's by a relative error of at most 0.0052.
Values may be sent and summed in bfloat16 or wider, within the bound.
No kernel may reach another device: no remote copies, remote signals or barrier semaphores. Data moves between devices by JAX's collectives and lax.ppermute only.
A program may use at most 64 MiB of HBM per device.

v0:
```python
import jax
import jax.numpy as jnp
from jax import lax
from jax.sharding import PartitionSpec as P

HEAD_DIM = 128
epsilon = 1e-06


def compensated(earlier, later):
    first_sum, first_comp = earlier
    second_sum, second_comp = later
    error_term = first_sum - (second_sum - second_sum) + (second_sum - second_sum)
    return (second_sum, error_term)


def fold_masked(heads_here, position, lower, running, portion):
    count = portion.shape[0] // heads_here
    owners = jnp.arange(count, dtype=jnp.int32)
    keep_mask = owners < position if lower else owners > position
    weights = keep_mask.astype(jnp.float32)
    blocks = portion.reshape((count, heads_here) + portion.shape[1:])
    added_part = jnp.sum(blocks * weights[:, None, None, None], axis=0)
    return compensated(running, (added_part, jnp.zeros_like(added_part)))


def body(queries, key_rows, value_rows, out_weight, cotangent):
    length = queries.shape[0]
    heads_here = queries.shape[1] // HEAD_DIM
    width_here = heads_here * HEAD_DIM
    highest = lax.Precision.HIGHEST
    query_three = queries.reshape(length, heads_here, HEAD_DIM)
    key_three = key_rows.reshape(length, heads_here, HEAD_DIM)
    value_three = value_rows.reshape(length, heads_here, HEAD_DIM)
    causal = lax.broadcasted_iota(jnp.int32, (length, length), 0) >= lax.broadcasted_iota(
        jnp.int32, (length, length), 1
    )
    position = lax.axis_index("ctx")
    scores = jnp.einsum("thd,shd->hts", query_three, key_three, preferred_element_type=jnp.float32)
    scores = jnp.where(causal[None], scores, 0.0).astype(jnp.bfloat16)
    block_state = jnp.einsum(
        "thd,the->hde", key_three, value_three, preferred_element_type=jnp.float32
    )
    zero_state = jnp.zeros_like(block_state)
    prefix_sums, prefix_comps = fold_masked(
        heads_here,
        position,
        True,
        (zero_state, zero_state),
        lax.all_gather(block_state, "ctx", axis=0, tiled=True),
    )
    prefix_state = prefix_sums + prefix_comps
    query_wide = query_three.astype(jnp.float32)
    attended = jnp.einsum("hts,she->the", scores, value_three, preferred_element_type=jnp.float32)
    attended = attended + jnp.einsum("thd,hde->the", query_wide, prefix_state, precision=highest)
    row_scale = lax.rsqrt(jnp.mean(attended * attended, axis=-1, keepdims=True) + epsilon)
    unit_rows = attended * row_scale
    normed = unit_rows.astype(jnp.bfloat16).reshape(length, width_here)
    partial_terms = jnp.dot(normed, out_weight, preferred_element_type=jnp.float32)
    mixed = lax.psum_scatter(partial_terms, "head", scatter_dimension=1, tiled=True).astype(
        jnp.bfloat16
    )
    full_grad = lax.all_gather(cotangent, "head", axis=1, tiled=True)
    upstream = lax.dot_general(
        full_grad, out_weight, (((1,), (1,)), ((), ())), preferred_element_type=jnp.float32
    )
    upstream = upstream.reshape(length, heads_here, HEAD_DIM)
    d_attended = row_scale * (
        upstream - unit_rows * jnp.mean(upstream * unit_rows, axis=-1, keepdims=True)
    )
    d_attended = d_attended.astype(jnp.bfloat16)
    grad_block = jnp.einsum(
        "thd,the->hde", query_three, d_attended, preferred_element_type=jnp.float32
    )
    suffix_sums, suffix_comps = fold_masked(
        heads_here,
        position,
        False,
        (zero_state, zero_state),
        lax.all_gather(grad_block, "ctx", axis=0, tiled=True),
    )
    suffix_state = suffix_sums + suffix_comps
    back_scores = jnp.einsum(
        "the,she->hts", d_attended, value_three, preferred_element_type=jnp.float32
    )
    back_scores = jnp.where(causal[None], back_scores, 0.0).astype(jnp.bfloat16)
    grad_wide = d_attended.astype(jnp.float32)
    grad_q = jnp.einsum("hts,shd->thd", back_scores, key_three, preferred_element_type=jnp.float32)
    grad_q = grad_q + jnp.einsum("the,hde->thd", grad_wide, prefix_state, precision=highest)
    grad_k = jnp.einsum(
        "hts,thd->shd", back_scores, query_three, preferred_element_type=jnp.float32
    )
    grad_k = grad_k + jnp.einsum(
        "she,hde->shd", value_three.astype(jnp.float32), suffix_state, precision=highest
    )
    grad_v = jnp.einsum("hts,the->she", scores, d_attended, preferred_element_type=jnp.float32)
    grad_v = grad_v + jnp.einsum(
        "shd,hde->she", key_three.astype(jnp.float32), suffix_state, precision=highest
    )
    grad_cols = lax.all_to_all(full_grad, "ctx", split_axis=1, concat_axis=0, tiled=True)
    grad_out_weight = lax.dot_general(
        lax.all_gather(normed, "ctx", axis=0, tiled=True),
        grad_cols,
        (((0,), (0,)), ((), ())),
        preferred_element_type=jnp.float32,
    )
    return (
        mixed,
        grad_q.astype(jnp.bfloat16).reshape(length, width_here),
        grad_k.astype(jnp.bfloat16).reshape(length, width_here),
        grad_v.astype(jnp.bfloat16).reshape(length, width_here),
        grad_out_weight,
    )


def solution(mesh):
    return jax.shard_map(
        body,
        mesh=mesh,
        in_specs=(
            P("ctx", "head"),
            P("ctx", "head"),
            P("ctx", "head"),
            P("head", None),
            P("ctx", "head"),
        ),
        out_specs=(
            P("ctx", "head"),
            P("ctx", "head"),
            P("ctx", "head"),
            P("ctx", "head"),
            P("head", "ctx"),
        ),
        check_vma=False,
    )
```

profile of v0, /device:TPU:0, one launch (start us, length us, event | category | flops | bytes accessed | tf_op | source)
XLA Modules:
  0.0 284.7 jit_solution(707623122106704745)
XLA Ops:
  7.3 1.3 copy.103
  8.9 2.1 fusion.11
  11.1 1.0 copy.79
  12.7 1.0 copy-done.5
  13.7 1.5 convolution_bitcast_fusion.5
  15.1 35.4 %all-gather.5.cloned.1.call-done = f32[64,128,128]{2,1,0:T(8,128)} async-done(((f32[8,128,128]{2,1,0:T(8,128)}), f32[64,128,128]{2,1,0:T(8,128)}) %all-gather.5.cloned.1.call-update) | async-done | bytes 4194320 | tf_op jit(solution)/shard_map/all_gather | solution.py:50
  50.5 2.8 multiply_reduce_fusion.1
  53.3 0.8 copy-done.2
  54.1 0.7 multiply_reduce_fusion.3
  54.9 43.5 %all-gather.7.cloned.1.call-done = bf16[256,4096]{0,1:T(8,128)(2,1)} async-done(((bf16[256,1024]{0,1:T(8,128)(2,1)}), bf16[256,4096]{0,1:T(8,128)(2,1)}) %all-gather.7.cloned.1.call-update) | async-done | bytes 2097168 | tf_op jit(solution)/shard_map/all_gather | solution.py:63
  98.3 6.3 %multiply_reduce_fusion.2 = (f32[256,8]{0,1:T(8,128)S(1)}, f32[256,1024]{0,1:T(8,128)S(1)}) fusion(f32[256,8,128]{0,2,1:T(8,128)S(1)} %get-tuple-element.28, f32[256,8]{0,1:T(8,128)S(1)} %add_rsqrt_fusion, bf16[1024,4096]{1,0:T(8,128)(2,1)} %param.8, bf16[256,4096]{0,1:T(8,128)(2,1)} %all-gather.7.cloned.1.call-done), kind=kOutput, calls=%fused_computation.19 | convolution fusion | flops 2148268032 | bytes 12599296 | tf_op jit(solution)/shard_map/dot_general | solution.py:64
  104.6 1.0 multiply_convert_fusion
  106.0 1.0 copy.87
  107.0 0.5 all-gather.11.cloned.1.call-update
  107.6 7.9 %fusion.41 = f32[256,4096]{1,0:T(8,128)} fusion(bf16[256,1024]{0,1:T(8,128)(2,1)} %bitcast.115, bf16[1024,4096]{1,0:T(8,128)(2,1)} %param.8), kind=kOutput, calls=%fused_computation.60 | convolution fusion | flops 2147483648 | bytes 13107200 | tf_op jit(solution)/shard_map/dot_general | solution.py:59
  115.6 4.6 %all-to-all-start = ((bf16[256,8,512]{0,2,1:T(8,128)(2,1)}), bf16[256,8,512]{0,2,1:T(8,128)(2,1)}, u32[]{:S(2)}, u32[]{:S(2)}) async-start(bf16[256,8,512]{0,2,1:T(8,128)(2,1)} %bitcast.15), calls=%async_computation.1 | async-start | bytes 4194304 | tf_op jit(solution)/shard_map/all_to_all | solution.py:100
  120.1 36.2 %all-to-all-done = bf16[256,8,512]{0,2,1:T(8,128)(2,1)} async-done(((bf16[256,8,512]{0,2,1:T(8,128)(2,1)}), bf16[256,8,512]{0,2,1:T(8,128)(2,1)}, u32[]{:S(2)}, u32[]{:S(2)}) %all-to-all-start) | async-done | bytes 2097184 | tf_op jit(solution)/shard_map/all_to_all | solution.py:100
  156.4 4.0 %copy.91 = bf16[8,256,512]{2,1,0:T(8,128)(2,1)} copy(bf16[8,256,512]{1,2,0:T(8,128)(2,1)} %bitcast.16) | data formatting | bytes 4194304 | tf_op jit(solution)/shard_map/all_to_all | solution.py:100
  160.3 0.5 select_convert_fusion
  161.3 0.6 fusion.3
  161.9 1.0 copy.92
  162.9 2.5 fusion.42
  165.4 1.7 convolution_bitcast_fusion.3
  167.2 3.0 %multiply_reduce_fusion = f32[8,128,128]{2,1,0:T(8,128)S(1)} fusion(f32[8,8,128,128]{3,2,1,0:T(8,128)} %bitcast.116, f32[8]{0:T(128)S(1)} %compare_convert_fusion), kind=kLoop, calls=%fused_computation | loop fusion | flops 1966080 | bytes 4718624 | tf_op jit(solution)/shard_map/reduce_sum | solution.py:23
  170.2 1.4 fusion.5
  171.6 2.0 copy.94
  173.7 0.6 fusion.4
  174.3 1.0 copy.93
  175.3 21.8 %all-gather.11.cloned.1.call-done = bf16[2048,1024]{0,1:T(8,128)(2,1)} async-done(((bf16[256,1024]{0,1:T(8,128)(2,1)}), bf16[2048,1024]{0,1:T(8,128)(2,1)}) %all-gather.11.cloned.1.call-update) | async-done | bytes 4194320 | tf_op jit(solution)/shard_map/all_gather | solution.py:102
  197.1 6.5 %fusion.43 = f32[1024,512]{1,0:T(8,128)} fusion(bf16[2048,1024]{0,1:T(8,128)(2,1)} %all-gather.11.cloned.1.call-done, bf16[2048,512]{1,0:T(8,128)(2,1)} %bitcast.122), kind=kOutput, calls=%fused_computation.62 | convolution fusion | flops 2147483648 | bytes 8388608 | tf_op jit(solution)/shard_map/dot_general | solution.py:101
  203.6 72.5 %reduce-scatter.2.cloned.1.call-done = f32[256,1024]{1,0:T(8,128)} async-done(((f32[256,4096]{1,0:T(8,128)}), f32[256,1024]{1,0:T(8,128)}) %reduce-scatter.2.cloned.1.call-update) | async-done | bytes 1048592 | tf_op jit(solution)/shard_map/reduce_scatter | solution.py:60
  276.1 2.1 convert_element_type.48
  (39 shorter events, 1.9 us)
Async XLA Ops:
  7.2 5.0 %copy-start = (bf16[256,1024]{1,0:T(8,128)(2,1)S(1)}, bf16[256,1024]{1,0:T(8,128)(2,1)}, u32[]{:S(2)}) copy-start(bf16[256,1024]{1,0:T(8,128)(2,1)} %param.5) | copy-start | bytes 1572868
  7.2 5.0 %copy-start.8 = (bf16[256,1024]{1,0:T(8,128)(2,1)S(1)}, bf16[256,1024]{1,0:T(8,128)(2,1)}, u32[]{:S(2)}) copy-start(bf16[256,1024]{1,0:T(8,128)(2,1)} %param.6) | copy-start | bytes 1572868
  7.2 3.9 %copy-start.10 = (bf16[256,1024]{1,0:T(8,128)(2,1)S(1)}, bf16[256,1024]{1,0:T(8,128)(2,1)}, u32[]{:S(2)}) copy-start(bf16[256,1024]{1,0:T(8,128)(2,1)} %param.9) | copy-start | bytes 1572868
  7.2 43.3 %all-gather.5.cloned.1.call-start = ((), (), s32[]{:S(2)}) async-start(), calls=%async_computation.2 | async-start | bytes 4718592 | tf_op jit(solution)/shard_map/all_gather | solution.py:50
  7.2 6.4 %copy-start.1 = (bf16[256,1024]{1,0:T(8,128)(2,1)S(1)}, bf16[256,1024]{1,0:T(8,128)(2,1)}, u32[]{:S(2)}) copy-start(bf16[256,1024]{1,0:T(8,128)(2,1)} %param.7) | copy-start | bytes 1572868
  11.0 87.3 %all-gather.7.cloned.1.call-start = ((), (), s32[]{:S(2)}) async-start(), calls=%async_computation.4 | async-start | bytes 2621440 | tf_op jit(solution)/shard_map/all_gather | solution.py:63
  12.1 155.0 %all-gather.9.cloned.1.call-start = ((), (), s32[]{:S(2)}) async-start(), calls=%async_computation.5 | async-start | bytes 4718592 | tf_op jit(solution)/shard_map/all_gather | solution.py:80
  12.7 1.0 copy-start.5
  50.5 3.6 %copy-start.4 = (f32[256,8,128]{0,2,1:T(8,128)S(1)}, f32[256,8,128]{0,2,1:T(8,128)}, u32[]{:S(2)}) copy-start(f32[256,8,128]{0,2,1:T(8,128)} %convolution_bitcast_fusion.5) | copy-start | bytes 3145732
  53.3 0.8 copy-start.2
  107.0 90.1 %all-gather.11.cloned.1.call-start = ((), (), s32[]{:S(2)}) async-start(), calls=%async_computation.6 | async-start | bytes 4718592 | tf_op jit(solution)/shard_map/all_gather | solution.py:102
  107.6 168.5 %reduce-scatter.2.cloned.1.call-start = ((), (), s32[]{:S(2)}) async-start(), calls=%async_computation.3 | async-start | bytes 5242880 | tf_op jit(solution)/shard_map/reduce_scatter | solution.py:60
  115.6 40.8 %all-to-all-start = ((bf16[256,8,512]{0,2,1:T(8,128)(2,1)}), bf16[256,8,512]{0,2,1:T(8,128)(2,1)}, u32[]{:S(2)}, u32[]{:S(2)}) async-start(bf16[256,8,512]{0,2,1:T(8,128)(2,1)} %bitcast.15), calls=%async_computation.1 | async-start | bytes 4194304 | tf_op jit(solution)/shard_map/all_to_all | solution.py:100
  156.4 4.9 %copy-start.3 = (f32[8,128,128]{2,1,0:T(8,128)S(1)}, f32[8,128,128]{2,1,0:T(8,128)}, u32[]{:S(2)}) copy-start(f32[8,128,128]{2,1,0:T(8,128)} %copy-done.2) | copy-start | bytes 1572868
  160.8 1.1 copy-start.6
  165.4 4.7 %copy-start.9 = (bf16[256,1024]{1,0:T(8,128)(2,1)S(1)}, bf16[256,1024]{1,0:T(8,128)(2,1)}, u32[]{:S(2)}) copy-start(bf16[256,1024]{1,0:T(8,128)(2,1)} %param.6) | copy-start | bytes 1572868
  167.2 3.0 %copy-start.7 = (f32[8,128,256]{2,1,0:T(8,128)S(1)}, f32[8,128,256]{2,1,0:T(8,128)}, u32[]{:S(2)}) copy-start(f32[8,128,256]{2,1,0:T(8,128)} %fusion.42) | copy-start | bytes 3145732
Sparse Core Ops, SparseCore 0:
  11.1 39.2 all-gather.4
  52.6 45.6 all-gather.6
  107.1 51.2 all-gather.8
  160.8 36.3 all-gather.10
  199.2 76.7 reduce-scatter.1
where the time goes:
time: 285 us
  waiting for transfers between devices  210 us (74%)
  matrix products  33.5 us (12%)
  between operations  14 us (5%)
  local copies, waits for them, and re-layouts  13.4 us (5%)
  other arithmetic  9 us (3%)
  starting transfers between devices  4.77 us (2%)
    reduce_scatter x1, waiting for transfers between devices, body(): lax.psum_scatter(partial_terms, 'head', scatter_dimension=1, tiled=True)  72.5 us
    all_gather x1, waiting for transfers between devices, body(): full_grad = lax.all_gather(cotangent, 'head', axis=1, tiled=True)  43.5 us
    all_to_all x1, waiting for transfers between devices, body(): lax.all_to_all(full_grad, 'ctx', split_axis=1, concat_axis=0, tiled=True)  36.2 us
    all_gather x1, waiting for transfers between devices, body(): lax.all_gather(block_state, 'ctx', axis=0, tiled=True)  35.4 us
    all_gather x1, waiting for transfers between devices, body(): lax.all_gather(normed, 'ctx', axis=0, tiled=True)  21.8 us
    unnamed x27, local copies, waits for them, and re-layouts  8.13 us
    dot_general x1, matrix products, body(): jnp.dot(normed, out_weight, preferred_element_type=jnp.float32)  7.92 us
    dot_general x1, matrix products, body(): lax.dot_general(lax.all_gather(normed, 'ctx', axis=0, tiled=True), grad_c...  6.51 us
  transfers between devices with their start and end apart: 6, of which 5 were waited for; matrix products, arithmetic and copies ran while one was open for 14% of the time, Pallas kernels for 0%

commit v1 on v0

--- a/solution.py
+++ b/solution.py
@@ -97,7 +97,10 @@
     grad_v = grad_v + jnp.einsum(
         "shd,hde->she", key_three.astype(jnp.float32), suffix_state, precision=highest
     )
-    grad_cols = lax.all_to_all(full_grad, "ctx", split_axis=1, concat_axis=0, tiled=True)
+    grad_cols = jnp.concatenate(
+        lax.all_to_all(jnp.stack(jnp.split(full_grad, lax.axis_size("ctx"), axis=1)), "ctx", 0, 0),
+        axis=0,
+    )
     grad_out_weight = lax.dot_general(
         lax.all_gather(normed, "ctx", axis=0, tiled=True),
         grad_cols,

time: 285 us -> 290 us (1.018)
  waiting for transfers between devices: 210 us -> 219 us
  matrix products: 33.5 us -> 28.1 us
    all_to_all x1, waiting for transfers between devices: 36.2 us -> 0.01 us  [body(): lax.all_to_all(jnp.stack(jnp.split(full_grad, lax.axis_size('ctx'), axis=...]
    all_gather x1, waiting for transfers between devices: 0.02 us -> 26.7 us  [body(): lax.all_gather(grad_block, 'ctx', axis=0, tiled=True)]
    all_gather x1, waiting for transfers between devices: 21.8 us -> 38.3 us  [body(): lax.all_gather(normed, 'ctx', axis=0, tiled=True)]
    unnamed x27 -> x43, local copies, waits for them, and re-layouts: 8.13 us -> 13.2 us
    all_to_all x1 -> x0, local copies, waits for them, and re-layouts: 3.97 us -> none  [body(): lax.all_to_all(full_grad, 'ctx', split_axis=1, concat_axis=0, tiled=True)]
  transfers between devices with their start and end apart: 6 -> 6, of which waited for: 5 -> 5; matrix products, arithmetic and copies ran while one was open for 14% -> 12% of each run, Pallas kernels for 0% -> 0%
where the time goes in v1:
time: 290 us
  waiting for transfers between devices  219 us (76%)
  matrix products  28.1 us (10%)
  local copies, waits for them, and re-layouts  15.3 us (5%)
  between operations  14.1 us (5%)
  other arithmetic  8.77 us (3%)
  starting transfers between devices  4.89 us (2%)
    reduce_scatter x1, waiting for transfers between devices, body(): lax.psum_scatter(partial_terms, 'head', scatter_dimension=1, tiled=True)  72.5 us
    all_gather x1, waiting for transfers between devices, body(): full_grad = lax.all_gather(cotangent, 'head', axis=1, tiled=True)  43 us
    all_gather x1, waiting for transfers between devices, body(): lax.all_gather(normed, 'ctx', axis=0, tiled=True)  38.3 us
    all_gather x1, waiting for transfers between devices, body(): lax.all_gather(block_state, 'ctx', axis=0, tiled=True)  37.1 us
    all_gather x1, waiting for transfers between devices, body(): lax.all_gather(grad_block, 'ctx', axis=0, tiled=True)  26.7 us
    unnamed x43, local copies, waits for them, and re-layouts  13.2 us
    dot_general x1, matrix products, body(): jnp.dot(normed, out_weight, preferred_element_type=jnp.float32)  7.71 us
    dot_general x1, matrix products, body(): lax.dot_general(lax.all_gather(normed, 'ctx', axis=0, tiled=True), grad_c...  6.51 us
  transfers between devices with their start and end apart: 6, of which 5 were waited for; matrix products, arithmetic and copies ran while one was open for 12% of the time, Pallas kernels for 0%

profile of v1, /device:TPU:0, one launch (start us, length us, event | category | flops | bytes accessed | tf_op | source)
XLA Modules:
  0.0 289.9 jit_solution(9388224912259749429)
XLA Ops:
  7.2 1.2 copy.59
  8.8 1.1 fusion.11
  11.3 1.0 copy-done.9
  12.7 37.1 %all-gather.5.cloned.1.call-done = f32[64,128,128]{2,1,0:T(8,128)} async-done(((f32[8,128,128]{2,1,0:T(8,128)}), f32[64,128,128]{2,1,0:T(8,128)}) %all-gather.5.cloned.1.call-update) | async-done | bytes 4194320 | tf_op jit(solution)/shard_map/all_gather | solution.py:50
  49.8 2.8 multiply_reduce_fusion.1
  52.6 0.8 copy-done.7
  53.4 0.7 multiply_reduce_fusion.3
  54.1 43.0 %all-gather.7.cloned.1.call-done = bf16[256,4096]{1,0:T(8,128)(2,1)} async-done(((bf16[256,1024]{1,0:T(8,128)(2,1)}), bf16[256,4096]{1,0:T(8,128)(2,1)}) %all-gather.7.cloned.1.call-update) | async-done | bytes 2097168 | tf_op jit(solution)/shard_map/all_gather | solution.py:63
  97.1 6.4 %multiply_reduce_fusion.2 = (f32[256,8]{0,1:T(8,128)S(1)}, f32[256,1024]{0,1:T(8,128)S(1)}) fusion(f32[256,8,128]{0,2,1:T(8,128)S(1)} %get-tuple-element.18, f32[256,8]{0,1:T(8,128)S(1)} %add_rsqrt_fusion, bf16[256,4096]{1,0:T(8,128)(2,1)} %all-gather.7.cloned.1.call-done, bf16[1024,4096]{1,0:T(8,128)(2,1)} %param.8), kind=kOutput, calls=%fused_computation.19 | convolution fusion | flops 2148268032 | bytes 12599296 | tf_op jit(solution)/shard_map/dot_general | solution.py:64
  103.5 1.0 multiply_convert_fusion
  104.8 1.0 copy.44
  106.5 7.7 %fusion.49 = f32[256,4096]{1,0:T(8,128)} fusion(bf16[256,1024]{0,1:T(8,128)(2,1)S(1)} %bitcast.145, bf16[1024,4096]{1,0:T(8,128)(2,1)} %param.8), kind=kOutput, calls=%fused_computation.76 | convolution fusion | flops 2147483648 | bytes 13107200 | tf_op jit(solution)/shard_map/dot_general | solution.py:59
  114.2 1.6 copy-done.1
  115.8 0.7 fusion.40
  116.5 0.7 fusion.39
  117.2 0.7 fusion.38
  117.9 0.7 fusion.37
  118.6 0.7 fusion.36
  119.4 0.7 fusion.35
  120.1 0.7 fusion.34
  120.8 0.7 fusion.33
  121.5 4.7 %all-to-all-start = ((bf16[8,256,512]{2,1,0:T(8,128)(2,1)}), bf16[8,256,512]{2,1,0:T(8,128)(2,1)}, u32[]{:S(2)}, u32[]{:S(2)}) async-start(bf16[8,256,512]{2,1,0:T(8,128)(2,1)} %fusion.33), calls=%async_computation.1 | async-start | bytes 4194304 | tf_op jit(solution)/shard_map/all_to_all | solution.py:101
  128.4 1.0 copy.48
  129.5 1.3 fusion.50
  131.1 26.7 %all-gather.9.cloned.1.call-done = f32[64,128,128]{2,1,0:T(8,128)} async-done(((f32[8,128,128]{2,1,0:T(8,128)}), f32[64,128,128]{2,1,0:T(8,128)}) %all-gather.9.cloned.1.call-update) | async-done | bytes 4194320 | tf_op jit(solution)/shard_map/all_gather | solution.py:80
  157.8 2.9 multiply_reduce_fusion
  161.4 1.0 copy.50
  163.0 1.0 copy.49
  164.0 38.3 %all-gather.11.cloned.1.call-done = bf16[2048,1024]{0,1:T(8,128)(2,1)} async-done(((bf16[256,1024]{0,1:T(8,128)(2,1)}), bf16[2048,1024]{0,1:T(8,128)(2,1)}) %all-gather.11.cloned.1.call-update) | async-done | bytes 4194320 | tf_op jit(solution)/shard_map/all_gather | solution.py:105
  202.3 6.5 %fusion.51 = f32[1024,512]{1,0:T(8,128)} fusion(bf16[2048,1024]{0,1:T(8,128)(2,1)} %all-gather.11.cloned.1.call-done, bf16[2048,512]{1,0:T(8,128)(2,1)} %bitcast.23), kind=kOutput, calls=%fused_computation.78 | convolution fusion | flops 2147483648 | bytes 8388608 | tf_op jit(solution)/shard_map/dot_general | solution.py:104
  208.9 72.5 %reduce-scatter.2.cloned.1.call-done = f32[256,1024]{1,0:T(8,128)} async-done(((f32[256,4096]{1,0:T(8,128)}), f32[256,1024]{1,0:T(8,128)}) %reduce-scatter.2.cloned.1.call-update) | async-done | bytes 1048592 | tf_op jit(solution)/shard_map/reduce_scatter | solution.py:60
  281.3 2.1 convert_element_type.48
  (55 shorter events, 6.9 us)
Async XLA Ops:
  7.2 3.6 %copy-start = (bf16[256,1024]{1,0:T(8,128)(2,1)S(1)}, bf16[256,1024]{1,0:T(8,128)(2,1)}, u32[]{:S(2)}) copy-start(bf16[256,1024]{1,0:T(8,128)(2,1)} %param.5) | copy-start | bytes 1572868
  7.2 1.6 copy-start.3
  7.2 42.6 %all-gather.5.cloned.1.call-start = ((), (), s32[]{:S(2)}) async-start(), calls=%async_computation.2 | async-start | bytes 4718592 | tf_op jit(solution)/shard_map/all_gather | solution.py:50
  8.5 2.3 copy-start.14
  8.8 2.4 copy-start.5
  9.9 87.1 %all-gather.7.cloned.1.call-start = ((), (), s32[]{:S(2)}) async-start(), calls=%async_computation.4 | async-start | bytes 2621440 | tf_op jit(solution)/shard_map/all_gather | solution.py:63
  10.7 147.1 %all-gather.9.cloned.1.call-start = ((), (), s32[]{:S(2)}) async-start(), calls=%async_computation.5 | async-start | bytes 4718592 | tf_op jit(solution)/shard_map/all_gather | solution.py:80
  11.3 1.0 copy-start.9
  52.6 0.8 copy-start.7
  104.5 1.9 copy-start.2
  105.8 96.5 %all-gather.11.cloned.1.call-start = ((), (), s32[]{:S(2)}) async-start(), calls=%async_computation.6 | async-start | bytes 4718592 | tf_op jit(solution)/shard_map/all_gather | solution.py:105
  106.4 174.9 %reduce-scatter.2.cloned.1.call-start = ((), (), s32[]{:S(2)}) async-start(), calls=%async_computation.3 | async-start | bytes 5242880 | tf_op jit(solution)/shard_map/reduce_scatter | solution.py:60
  114.2 1.6 copy-start.1
  121.5 4.7 %copy-start.4 = (bf16[256,1024]{1,0:T(8,128)(2,1)S(1)}, bf16[256,1024]{1,0:T(8,128)(2,1)}, u32[]{:S(2)}) copy-start(bf16[256,1024]{1,0:T(8,128)(2,1)} %param.7) | copy-start | bytes 1572868
  121.5 42.5 %all-to-all-start = ((bf16[8,256,512]{2,1,0:T(8,128)(2,1)}), bf16[8,256,512]{2,1,0:T(8,128)(2,1)}, u32[]{:S(2)}, u32[]{:S(2)}) async-start(bf16[8,256,512]{2,1,0:T(8,128)(2,1)} %fusion.33), calls=%async_computation.1 | async-start | bytes 4194304 | tf_op jit(solution)/shard_map/all_to_all | solution.py:101
  126.2 1.1 copy-start.6
  126.3 1.6 copy-start.8
  127.3 1.1 copy-start.11
  127.8 1.6 copy-start.10
  129.4 1.3 copy-start.12
  157.8 2.9 copy-start.13
  157.8 2.9 copy-start.15
Sparse Core Ops, SparseCore 0:
  10.5 39.2 all-gather.4
  51.4 45.6 all-gather.6
  105.9 51.8 all-gather.8
  160.1 42.1 all-gather.10
  204.5 76.7 reduce-scatter.1
